TPU v7x, 512 devices: a whole 4x8x8 slice. The times are simulated.
512 devices in a mesh: space: 64 (over z, x, y_lo), sta: 8 (over y_hi, core).
Axes of the slice: x: 4, y: 8 (y_hi: 4, y_lo: 2; y = y_hi * 2 + y_lo), z: 8, core: 2. Of those that a mesh axis runs over, the one named last changes fastest.
Arguments:
- coarse_times: float32 [16, 320, 32, 128], P('sta', 'space'), as said below
- model_map: int32 [320, 32, 128], P('space'), may hold values from 0 to 63
- slowness: float32 [64], replicated, may hold values from 0.12 to 0.3
- picks: float32 [256, 16], replicated
- pick_mask: int32 [256, 16], replicated, may hold values from 0 to 1, as said below
Outputs:
- refined: float32 [16, 320, 32, 128], P(None, 'space', 'sta')
- density: float32 [256, 320, 32, 128], P(None, 'space', 'sta')
Inputs may be any that keep to these rules, and one draw needn't show every extreme that they name: `pick_mask`: each event has at least 4 stations with a pick. `coarse_times`: zero at each station's own cell and positive elsewhere.
All inputs are finite; a program needn't handle non-finite values.
Results may differ from a plain program's by a relative error of at most 0.0003.
Values sent between devices are 32-bit elements; how exact they have to be, the bound alone decides.
A program may use at most 64 MiB of HBM per device.

v0:
```python
import jax
import jax.numpy as jnp
from jax import lax
from jax.sharding import PartitionSpec as P

ROUNDS = 12
BIG = 1000000.0
pick_sigma = 0.25
grid_step = 1.0
block_events = 32


def extended_2(block, sides, width):
    for axis, dim in sides:
        count = lax.axis_size(axis)
        forward = [(i, i + 1) for i in range(count - 1)]
        backward = [(target, source) for source, target in forward]
        low = lax.ppermute(
            lax.slice_in_dim(block, block.shape[dim] - width, None, axis=dim), axis, forward
        )
        high = lax.ppermute(lax.slice_in_dim(block, 0, width, axis=dim), axis, backward)
        block = jnp.concatenate([low, block, high], axis=dim)
    return block


def godunov(near_one, near_two, near_three, speed):
    lowest = jnp.minimum(jnp.minimum(near_one, near_two), near_three)
    highest = jnp.maximum(jnp.maximum(near_one, near_two), near_three)
    middle = jnp.maximum(
        jnp.minimum(near_one, near_two), jnp.minimum(jnp.maximum(near_one, near_two), near_three)
    )
    gap_mid = middle - lowest
    gap_high = highest - lowest
    two_sided = 0.5 * (
        gap_mid + jnp.sqrt(jnp.maximum(2.0 * speed * speed - gap_mid * gap_mid, 0.0))
    )
    gap_sum = gap_mid + gap_high
    squares = gap_mid * gap_mid + gap_high * gap_high - speed * speed
    three_sided = (gap_sum + jnp.sqrt(jnp.maximum(gap_sum * gap_sum - 3.0 * squares, 0.0))) / 3.0
    increase = jnp.where(
        speed <= gap_mid, speed, jnp.where(two_sided <= gap_high, two_sided, three_sided)
    )
    return lowest + increase


def relax(extended, speed):
    centre = extended[:, 1:-1]
    along_x = jnp.minimum(extended[:, :-2], extended[:, 2:])
    padded = jnp.pad(centre, ((0, 0), (0, 0), (1, 1), (1, 1)), constant_values=BIG)
    along_y = jnp.minimum(padded[:, :, :-2, 1:-1], padded[:, :, 2:, 1:-1])
    along_z = jnp.minimum(padded[:, :, 1:-1, :-2], padded[:, :, 1:-1, 2:])
    return jnp.minimum(centre, godunov(along_x, along_y, along_z, speed[None]))


def close_rims(extended, rim_width, at_lower, at_upper):
    cell_count = extended.shape[1]
    position = lax.broadcasted_iota(jnp.int32, (1, cell_count, 1, 1), 1)
    outside = (position < rim_width) & at_lower | (position >= cell_count - rim_width) & at_upper
    return jnp.where(outside, BIG, extended)


def misfit_block(event_pair, flat_tables):
    arrivals, observed = event_pair
    pick_count = jnp.sum(observed, 1)
    residual = arrivals[:, :, None] - flat_tables[None]
    anchor_shift = jnp.sum(observed[:, :, None] * residual, 1) / pick_count[:, None]
    deviation = residual - anchor_shift[:, None, :]
    return jnp.sum(observed[:, :, None] * deviation * deviation, 1)


def body(coarse_times, model_map, slowness, picks, pick_mask):
    levels = lax.broadcasted_iota(jnp.int32, (slowness.shape[0], 1, 1, 1), 0)
    speed = grid_step * jnp.sum(
        jnp.where(model_map[None] == levels, slowness[:, None, None, None], 0.0), 0
    )
    position_space = lax.axis_index("space")
    devices_space = lax.axis_size("space")
    at_lower = position_space == 0
    at_upper = position_space == devices_space - 1
    tables = coarse_times

    def one_round(round_index, tables):
        extended = extended_2(tables, (("space", 1),), 1)
        return relax(close_rims(extended, 1, at_lower, at_upper), speed)

    tables = lax.fori_loop(0, ROUNDS, one_round, tables)
    refined = lax.all_to_all(tables, "sta", split_axis=2, concat_axis=0, tiled=True)
    stations = refined.shape[0]
    flat_tables = refined.reshape(stations, -1)
    observed = pick_mask.astype(jnp.float32)
    blocks = lax.map(
        lambda event_pair: misfit_block(event_pair, flat_tables),
        (picks.reshape(-1, block_events, stations), observed.reshape(-1, block_events, stations)),
    )
    score = -0.5 * blocks.reshape(picks.shape[0], -1) / (pick_sigma * pick_sigma)
    local_top = jnp.max(score, 1)
    top_score = lax.pmax(local_top, ("space", "sta"))
    cell_weights = jnp.exp(score - top_score[:, None])
    mass_sum = lax.psum(jnp.sum(cell_weights, 1), ("space", "sta"))
    density = cell_weights / mass_sum[:, None]
    density = density.reshape(picks.shape[0], refined.shape[1], refined.shape[2], refined.shape[3])
    return (refined, density)


def solution(mesh):
    placed = (P("sta", "space", None, None), P("space", None, None), P(), P(), P())
    return jax.shard_map(
        body,
        mesh=mesh,
        in_specs=placed,
        out_specs=(P(None, "space", "sta", None), P(None, "space", "sta", None)),
        check_vma=False,
    )
```

profile of v0, /device:TPU:1, one launch (start us, length us, event | category | flops | bytes accessed | tf_op | source)
XLA Modules:
  0.0 400.3 jit_solution(15108687910519187585)
XLA Ops:
  1.5 1.5 select_reduce_fusion
  3.1 96.4 %while.22 = (s32[]{:T(128)}, f32[2,5,32,128]{3,2,1,0:T(8,128)S(1)}, pred[]{:T(512)}, pred[]{:T(512)}, f32[5,32,128]{2,1,0:T(8,128)S(1)}, /*index=5*/f32[1,5,32,128]{3,2,1,0:T(8,128)S(1)}, s32[]{:T(128)}) while((s32[]{:T(128)}, f32[2,5,32,128]{3,2,1,0:T(8,128)S(1)}, pred[]{:T(512)}, pred[]{:T(512)}, f32[5,32,128]{2,1,0:T(8,128)S(1)}, ...), condition=%wide.region_2.3_spmd, body=%wide.region_1.2_spmd.sunk | while | flops 1523749 | bytes 2244781 | solution.py:86
  3.1 1.3 collective-permute-start
  4.4 4.6 %collective-permute-start.1 = (f32[2,1,32,128]{3,2,1,0:T(8,128)S(1)}, f32[2,1,32,128]{3,2,1,0:T(8,128)S(1)}, u32[]{:S(2)}, u32[]{:S(2)}) collective-permute-start(f32[2,1,32,128]{3,2,1,0:T(8,128)S(1)} %get-tuple-element.226), channel_id=1, source_target_pairs={{0,8},{8,16},{16,24},{24,32},{32,40},{40,48},{48,56},{56,64},{64,7... | collective-permute-start | bytes 98312 | tf_op jit(solution)/shard_map/while/body/eval_jaxpr/ppermute | solution.py:18
  10.6 1.3 collective-permute-start
  11.9 4.9 %collective-permute-start.1 = (f32[2,1,32,128]{3,2,1,0:T(8,128)S(1)}, f32[2,1,32,128]{3,2,1,0:T(8,128)S(1)}, u32[]{:S(2)}, u32[]{:S(2)}) collective-permute-start(f32[2,1,32,128]{3,2,1,0:T(8,128)S(1)} %get-tuple-element.226), channel_id=1, source_target_pairs={{0,8},{8,16},{16,24},{24,32},{32,40},{40,48},{48,56},{56,64},{64,7... | collective-permute-start | bytes 98312 | tf_op jit(solution)/shard_map/while/body/eval_jaxpr/ppermute | solution.py:18
  19.5 5.2 %collective-permute-start.1 = (f32[2,1,32,128]{3,2,1,0:T(8,128)S(1)}, f32[2,1,32,128]{3,2,1,0:T(8,128)S(1)}, u32[]{:S(2)}, u32[]{:S(2)}) collective-permute-start(f32[2,1,32,128]{3,2,1,0:T(8,128)S(1)} %get-tuple-element.226), channel_id=1, source_target_pairs={{0,8},{8,16},{16,24},{24,32},{32,40},{40,48},{48,56},{56,64},{64,7... | collective-permute-start | bytes 98312 | tf_op jit(solution)/shard_map/while/body/eval_jaxpr/ppermute | solution.py:18
  27.5 5.2 %collective-permute-start.1 = (f32[2,1,32,128]{3,2,1,0:T(8,128)S(1)}, f32[2,1,32,128]{3,2,1,0:T(8,128)S(1)}, u32[]{:S(2)}, u32[]{:S(2)}) collective-permute-start(f32[2,1,32,128]{3,2,1,0:T(8,128)S(1)} %get-tuple-element.226), channel_id=1, source_target_pairs={{0,8},{8,16},{16,24},{24,32},{32,40},{40,48},{48,56},{56,64},{64,7... | collective-permute-start | bytes 98312 | tf_op jit(solution)/shard_map/while/body/eval_jaxpr/ppermute | solution.py:18
  35.5 5.2 %collective-permute-start.1 = (f32[2,1,32,128]{3,2,1,0:T(8,128)S(1)}, f32[2,1,32,128]{3,2,1,0:T(8,128)S(1)}, u32[]{:S(2)}, u32[]{:S(2)}) collective-permute-start(f32[2,1,32,128]{3,2,1,0:T(8,128)S(1)} %get-tuple-element.226), channel_id=1, source_target_pairs={{0,8},{8,16},{16,24},{24,32},{32,40},{40,48},{48,56},{56,64},{64,7... | collective-permute-start | bytes 98312 | tf_op jit(solution)/shard_map/while/body/eval_jaxpr/ppermute | solution.py:18
  43.4 5.2 %collective-permute-start.1 = (f32[2,1,32,128]{3,2,1,0:T(8,128)S(1)}, f32[2,1,32,128]{3,2,1,0:T(8,128)S(1)}, u32[]{:S(2)}, u32[]{:S(2)}) collective-permute-start(f32[2,1,32,128]{3,2,1,0:T(8,128)S(1)} %get-tuple-element.226), channel_id=1, source_target_pairs={{0,8},{8,16},{16,24},{24,32},{32,40},{40,48},{48,56},{56,64},{64,7... | collective-permute-start | bytes 98312 | tf_op jit(solution)/shard_map/while/body/eval_jaxpr/ppermute | solution.py:18
  51.4 5.2 %collective-permute-start.1 = (f32[2,1,32,128]{3,2,1,0:T(8,128)S(1)}, f32[2,1,32,128]{3,2,1,0:T(8,128)S(1)}, u32[]{:S(2)}, u32[]{:S(2)}) collective-permute-start(f32[2,1,32,128]{3,2,1,0:T(8,128)S(1)} %get-tuple-element.226), channel_id=1, source_target_pairs={{0,8},{8,16},{16,24},{24,32},{32,40},{40,48},{48,56},{56,64},{64,7... | collective-permute-start | bytes 98312 | tf_op jit(solution)/shard_map/while/body/eval_jaxpr/ppermute | solution.py:18
  59.4 5.2 %collective-permute-start.1 = (f32[2,1,32,128]{3,2,1,0:T(8,128)S(1)}, f32[2,1,32,128]{3,2,1,0:T(8,128)S(1)}, u32[]{:S(2)}, u32[]{:S(2)}) collective-permute-start(f32[2,1,32,128]{3,2,1,0:T(8,128)S(1)} %get-tuple-element.226), channel_id=1, source_target_pairs={{0,8},{8,16},{16,24},{24,32},{32,40},{40,48},{48,56},{56,64},{64,7... | collective-permute-start | bytes 98312 | tf_op jit(solution)/shard_map/while/body/eval_jaxpr/ppermute | solution.py:18
  67.3 5.3 %collective-permute-start.1 = (f32[2,1,32,128]{3,2,1,0:T(8,128)S(1)}, f32[2,1,32,128]{3,2,1,0:T(8,128)S(1)}, u32[]{:S(2)}, u32[]{:S(2)}) collective-permute-start(f32[2,1,32,128]{3,2,1,0:T(8,128)S(1)} %get-tuple-element.226), channel_id=1, source_target_pairs={{0,8},{8,16},{16,24},{24,32},{32,40},{40,48},{48,56},{56,64},{64,7... | collective-permute-start | bytes 98312 | tf_op jit(solution)/shard_map/while/body/eval_jaxpr/ppermute | solution.py:18
  75.4 5.3 %collective-permute-start.1 = (f32[2,1,32,128]{3,2,1,0:T(8,128)S(1)}, f32[2,1,32,128]{3,2,1,0:T(8,128)S(1)}, u32[]{:S(2)}, u32[]{:S(2)}) collective-permute-start(f32[2,1,32,128]{3,2,1,0:T(8,128)S(1)} %get-tuple-element.226), channel_id=1, source_target_pairs={{0,8},{8,16},{16,24},{24,32},{32,40},{40,48},{48,56},{56,64},{64,7... | collective-permute-start | bytes 98312 | tf_op jit(solution)/shard_map/while/body/eval_jaxpr/ppermute | solution.py:18
  83.5 5.2 %collective-permute-start.1 = (f32[2,1,32,128]{3,2,1,0:T(8,128)S(1)}, f32[2,1,32,128]{3,2,1,0:T(8,128)S(1)}, u32[]{:S(2)}, u32[]{:S(2)}) collective-permute-start(f32[2,1,32,128]{3,2,1,0:T(8,128)S(1)} %get-tuple-element.226), channel_id=1, source_target_pairs={{0,8},{8,16},{16,24},{24,32},{32,40},{40,48},{48,56},{56,64},{64,7... | collective-permute-start | bytes 98312 | tf_op jit(solution)/shard_map/while/body/eval_jaxpr/ppermute | solution.py:18
  91.5 6.5 %collective-permute-start.1 = (f32[2,1,32,128]{3,2,1,0:T(8,128)S(1)}, f32[2,1,32,128]{3,2,1,0:T(8,128)S(1)}, u32[]{:S(2)}, u32[]{:S(2)}) collective-permute-start(f32[2,1,32,128]{3,2,1,0:T(8,128)S(1)} %get-tuple-element.226), channel_id=1, source_target_pairs={{0,8},{8,16},{16,24},{24,32},{32,40},{40,48},{48,56},{56,64},{64,7... | collective-permute-start | bytes 98312 | tf_op jit(solution)/shard_map/while/body/eval_jaxpr/ppermute | solution.py:18
  100.3 20.7 %all-to-all-start = ((f32[2,5,32,128]{3,0,1,2:T(2,128)}), f32[2,5,32,128]{3,0,1,2:T(2,128)S(1)}, u32[]{:S(2)}, u32[]{:S(2)}) async-start(f32[2,5,32,128]{3,0,1,2:T(2,128)} %copy.27), calls=%async_computation | async-start | bytes 327680 | tf_op jit(solution)/shard_map/all_to_all | solution.py:87
  121.2 8.6 %all-to-all-done = f32[2,5,32,128]{3,0,1,2:T(2,128)S(1)} async-done(((f32[2,5,32,128]{3,0,1,2:T(2,128)}), f32[2,5,32,128]{3,0,1,2:T(2,128)S(1)}, u32[]{:S(2)}, u32[]{:S(2)}) %all-to-all-start) | async-done | bytes 163872 | tf_op jit(solution)/shard_map/all_to_all | solution.py:87
  130.4 26.5 %while.23 = (s32[]{:T(128)}, f32[8,32,2560]{2,1,0:T(8,128)S(1)}, f32[8,32,16]{1,0,2:T(8,128)S(1)}, f32[8,32,16]{1,0,2:T(8,128)S(1)}, f32[16,5,4,128]{3,2,1,0:T(4...) while((s32[]{:T(128)}, f32[8,32,2560]{2,1,0:T(8,128)S(1)}, f32[8,32,16]{1,0,2:T(8,128)S(1)}, ...), condition=%wide.wide.region_7.8_spmd, body=%wide.wide.region_3.7_spmd.sunk | while | flops 10404322 | bytes 2648417 | solution.py:91
  131.9 1.8 fusion.18
  135.3 1.8 fusion.18
  138.6 1.8 fusion.18
  141.9 1.8 fusion.18
  145.2 1.8 fusion.18
  148.5 1.8 fusion.18
  151.8 1.8 fusion.18
  155.1 1.8 fusion.18
  157.3 141.2 %pmax.7 = f32[256]{0:T(256)S(1)} all-reduce(f32[256]{0:T(256)S(1)} %reduce_max.12), channel_id=1, replica_groups=mesh['space'=64,'sta'=8] {'space','sta'}, use_global_device_ids=true, to_apply=%region_9.10 | all-reduce | flops 256 | bytes 2048 | tf_op jit(solution)/shard_map/pmax | solution.py:97
  298.5 2.0 exponential_reduce_fusion
  300.5 2.8 div.34
  303.4 94.4 %psum.7 = f32[256]{0:T(256)S(1)} all-reduce(f32[256]{0:T(256)S(1)} %reduce_sum.49), channel_id=1, replica_groups=mesh['space'=64,'sta'=8] {'space','sta'}, use_global_device_ids=true, to_apply=%region_11.12 | all-reduce | flops 256 | bytes 2048 | tf_op jit(solution)/shard_map/psum | solution.py:99
  397.8 2.5 exponential_divide_fusion
  (181 shorter events, 45.1 us)
Async XLA Ops:
  3.1 117.9 %copy-start.2 = (s32[256,16]{0,1:T(8,128)S(1)}, s32[256,16]{0,1:T(8,128)}, u32[]{:S(2)}) copy-start(s32[256,16]{0,1:T(8,128)} %param.13) | copy-start | bytes 49156
  3.1 118.0 %copy-start.1 = (f32[256,16]{0,1:T(8,128)S(1)}, f32[256,16]{0,1:T(8,128)}, u32[]{:S(2)}) copy-start(f32[256,16]{0,1:T(8,128)} %param.12) | copy-start | bytes 49156
  3.1 6.0 %collective-permute-start = (f32[2,1,32,128]{3,2,1,0:T(8,128)S(1)}, f32[2,1,32,128]{3,2,1,0:T(8,128)S(1)}, u32[]{:S(2)}, u32[]{:S(2)}) collective-permute-start(f32[2,1,32,128]{3,2,1,0:T(8,128)S(1)} %get-tuple-element.225), channel_id=1, source_target_pairs={{8,0},{16,8},{24,16},{32,24},{40,32},{48,40},{56,48},{64,56},{72,6... | collective-permute-start | bytes 98312 | tf_op jit(solution)/shard_map/while/body/eval_jaxpr/ppermute | solution.py:21
  4.4 5.7 %collective-permute-start.1 = (f32[2,1,32,128]{3,2,1,0:T(8,128)S(1)}, f32[2,1,32,128]{3,2,1,0:T(8,128)S(1)}, u32[]{:S(2)}, u32[]{:S(2)}) collective-permute-start(f32[2,1,32,128]{3,2,1,0:T(8,128)S(1)} %get-tuple-element.226), channel_id=1, source_target_pairs={{0,8},{8,16},{16,24},{24,32},{32,40},{40,48},{48,56},{56,64},{64,7... | collective-permute-start | bytes 98312 | tf_op jit(solution)/shard_map/while/body/eval_jaxpr/ppermute | solution.py:18
  10.6 6.2 %collective-permute-start = (f32[2,1,32,128]{3,2,1,0:T(8,128)S(1)}, f32[2,1,32,128]{3,2,1,0:T(8,128)S(1)}, u32[]{:S(2)}, u32[]{:S(2)}) collective-permute-start(f32[2,1,32,128]{3,2,1,0:T(8,128)S(1)} %get-tuple-element.225), channel_id=1, source_target_pairs={{8,0},{16,8},{24,16},{32,24},{40,32},{48,40},{56,48},{64,56},{72,6... | collective-permute-start | bytes 98312 | tf_op jit(solution)/shard_map/while/body/eval_jaxpr/ppermute | solution.py:21
  11.9 5.9 %collective-permute-start.1 = (f32[2,1,32,128]{3,2,1,0:T(8,128)S(1)}, f32[2,1,32,128]{3,2,1,0:T(8,128)S(1)}, u32[]{:S(2)}, u32[]{:S(2)}) collective-permute-start(f32[2,1,32,128]{3,2,1,0:T(8,128)S(1)} %get-tuple-element.226), channel_id=1, source_target_pairs={{0,8},{8,16},{16,24},{24,32},{32,40},{40,48},{48,56},{56,64},{64,7... | collective-permute-start | bytes 98312 | tf_op jit(solution)/shard_map/while/body/eval_jaxpr/ppermute | solution.py:18
  18.2 6.5 %collective-permute-start = (f32[2,1,32,128]{3,2,1,0:T(8,128)S(1)}, f32[2,1,32,128]{3,2,1,0:T(8,128)S(1)}, u32[]{:S(2)}, u32[]{:S(2)}) collective-permute-start(f32[2,1,32,128]{3,2,1,0:T(8,128)S(1)} %get-tuple-element.225), channel_id=1, source_target_pairs={{8,0},{16,8},{24,16},{32,24},{40,32},{48,40},{56,48},{64,56},{72,6... | collective-permute-start | bytes 98312 | tf_op jit(solution)/shard_map/while/body/eval_jaxpr/ppermute | solution.py:21
  19.5 6.2 %collective-permute-start.1 = (f32[2,1,32,128]{3,2,1,0:T(8,128)S(1)}, f32[2,1,32,128]{3,2,1,0:T(8,128)S(1)}, u32[]{:S(2)}, u32[]{:S(2)}) collective-permute-start(f32[2,1,32,128]{3,2,1,0:T(8,128)S(1)} %get-tuple-element.226), channel_id=1, source_target_pairs={{0,8},{8,16},{16,24},{24,32},{32,40},{40,48},{48,56},{56,64},{64,7... | collective-permute-start | bytes 98312 | tf_op jit(solution)/shard_map/while/body/eval_jaxpr/ppermute | solution.py:18
  26.2 6.5 %collective-permute-start = (f32[2,1,32,128]{3,2,1,0:T(8,128)S(1)}, f32[2,1,32,128]{3,2,1,0:T(8,128)S(1)}, u32[]{:S(2)}, u32[]{:S(2)}) collective-permute-start(f32[2,1,32,128]{3,2,1,0:T(8,128)S(1)} %get-tuple-element.225), channel_id=1, source_target_pairs={{8,0},{16,8},{24,16},{32,24},{40,32},{48,40},{56,48},{64,56},{72,6... | collective-permute-start | bytes 98312 | tf_op jit(solution)/shard_map/while/body/eval_jaxpr/ppermute | solution.py:21
  27.5 6.2 %collective-permute-start.1 = (f32[2,1,32,128]{3,2,1,0:T(8,128)S(1)}, f32[2,1,32,128]{3,2,1,0:T(8,128)S(1)}, u32[]{:S(2)}, u32[]{:S(2)}) collective-permute-start(f32[2,1,32,128]{3,2,1,0:T(8,128)S(1)} %get-tuple-element.226), channel_id=1, source_target_pairs={{0,8},{8,16},{16,24},{24,32},{32,40},{40,48},{48,56},{56,64},{64,7... | collective-permute-start | bytes 98312 | tf_op jit(solution)/shard_map/while/body/eval_jaxpr/ppermute | solution.py:18
  34.2 6.5 %collective-permute-start = (f32[2,1,32,128]{3,2,1,0:T(8,128)S(1)}, f32[2,1,32,128]{3,2,1,0:T(8,128)S(1)}, u32[]{:S(2)}, u32[]{:S(2)}) collective-permute-start(f32[2,1,32,128]{3,2,1,0:T(8,128)S(1)} %get-tuple-element.225), channel_id=1, source_target_pairs={{8,0},{16,8},{24,16},{32,24},{40,32},{48,40},{56,48},{64,56},{72,6... | collective-permute-start | bytes 98312 | tf_op jit(solution)/shard_map/while/body/eval_jaxpr/ppermute | solution.py:21
  35.5 6.2 %collective-permute-start.1 = (f32[2,1,32,128]{3,2,1,0:T(8,128)S(1)}, f32[2,1,32,128]{3,2,1,0:T(8,128)S(1)}, u32[]{:S(2)}, u32[]{:S(2)}) collective-permute-start(f32[2,1,32,128]{3,2,1,0:T(8,128)S(1)} %get-tuple-element.226), channel_id=1, source_target_pairs={{0,8},{8,16},{16,24},{24,32},{32,40},{40,48},{48,56},{56,64},{64,7... | collective-permute-start | bytes 98312 | tf_op jit(solution)/shard_map/while/body/eval_jaxpr/ppermute | solution.py:18
  42.1 6.5 %collective-permute-start = (f32[2,1,32,128]{3,2,1,0:T(8,128)S(1)}, f32[2,1,32,128]{3,2,1,0:T(8,128)S(1)}, u32[]{:S(2)}, u32[]{:S(2)}) collective-permute-start(f32[2,1,32,128]{3,2,1,0:T(8,128)S(1)} %get-tuple-element.225), channel_id=1, source_target_pairs={{8,0},{16,8},{24,16},{32,24},{40,32},{48,40},{56,48},{64,56},{72,6... | collective-permute-start | bytes 98312 | tf_op jit(solution)/shard_map/while/body/eval_jaxpr/ppermute | solution.py:21
  43.4 6.2 %collective-permute-start.1 = (f32[2,1,32,128]{3,2,1,0:T(8,128)S(1)}, f32[2,1,32,128]{3,2,1,0:T(8,128)S(1)}, u32[]{:S(2)}, u32[]{:S(2)}) collective-permute-start(f32[2,1,32,128]{3,2,1,0:T(8,128)S(1)} %get-tuple-element.226), channel_id=1, source_target_pairs={{0,8},{8,16},{16,24},{24,32},{32,40},{40,48},{48,56},{56,64},{64,7... | collective-permute-start | bytes 98312 | tf_op jit(solution)/shard_map/while/body/eval_jaxpr/ppermute | solution.py:18
  50.1 6.5 %collective-permute-start = (f32[2,1,32,128]{3,2,1,0:T(8,128)S(1)}, f32[2,1,32,128]{3,2,1,0:T(8,128)S(1)}, u32[]{:S(2)}, u32[]{:S(2)}) collective-permute-start(f32[2,1,32,128]{3,2,1,0:T(8,128)S(1)} %get-tuple-element.225), channel_id=1, source_target_pairs={{8,0},{16,8},{24,16},{32,24},{40,32},{48,40},{56,48},{64,56},{72,6... | collective-permute-start | bytes 98312 | tf_op jit(solution)/shard_map/while/body/eval_jaxpr/ppermute | solution.py:21
  51.4 6.2 %collective-permute-start.1 = (f32[2,1,32,128]{3,2,1,0:T(8,128)S(1)}, f32[2,1,32,128]{3,2,1,0:T(8,128)S(1)}, u32[]{:S(2)}, u32[]{:S(2)}) collective-permute-start(f32[2,1,32,128]{3,2,1,0:T(8,128)S(1)} %get-tuple-element.226), channel_id=1, source_target_pairs={{0,8},{8,16},{16,24},{24,32},{32,40},{40,48},{48,56},{56,64},{64,7... | collective-permute-start | bytes 98312 | tf_op jit(solution)/shard_map/while/body/eval_jaxpr/ppermute | solution.py:18
  58.1 6.5 %collective-permute-start = (f32[2,1,32,128]{3,2,1,0:T(8,128)S(1)}, f32[2,1,32,128]{3,2,1,0:T(8,128)S(1)}, u32[]{:S(2)}, u32[]{:S(2)}) collective-permute-start(f32[2,1,32,128]{3,2,1,0:T(8,128)S(1)} %get-tuple-element.225), channel_id=1, source_target_pairs={{8,0},{16,8},{24,16},{32,24},{40,32},{48,40},{56,48},{64,56},{72,6... | collective-permute-start | bytes 98312 | tf_op jit(solution)/shard_map/while/body/eval_jaxpr/ppermute | solution.py:21
  59.4 6.2 %collective-permute-start.1 = (f32[2,1,32,128]{3,2,1,0:T(8,128)S(1)}, f32[2,1,32,128]{3,2,1,0:T(8,128)S(1)}, u32[]{:S(2)}, u32[]{:S(2)}) collective-permute-start(f32[2,1,32,128]{3,2,1,0:T(8,128)S(1)} %get-tuple-element.226), channel_id=1, source_target_pairs={{0,8},{8,16},{16,24},{24,32},{32,40},{40,48},{48,56},{56,64},{64,7... | collective-permute-start | bytes 98312 | tf_op jit(solution)/shard_map/while/body/eval_jaxpr/ppermute | solution.py:18
  66.0 6.6 %collective-permute-start = (f32[2,1,32,128]{3,2,1,0:T(8,128)S(1)}, f32[2,1,32,128]{3,2,1,0:T(8,128)S(1)}, u32[]{:S(2)}, u32[]{:S(2)}) collective-permute-start(f32[2,1,32,128]{3,2,1,0:T(8,128)S(1)} %get-tuple-element.225), channel_id=1, source_target_pairs={{8,0},{16,8},{24,16},{32,24},{40,32},{48,40},{56,48},{64,56},{72,6... | collective-permute-start | bytes 98312 | tf_op jit(solution)/shard_map/while/body/eval_jaxpr/ppermute | solution.py:21
  67.3 6.3 %collective-permute-start.1 = (f32[2,1,32,128]{3,2,1,0:T(8,128)S(1)}, f32[2,1,32,128]{3,2,1,0:T(8,128)S(1)}, u32[]{:S(2)}, u32[]{:S(2)}) collective-permute-start(f32[2,1,32,128]{3,2,1,0:T(8,128)S(1)} %get-tuple-element.226), channel_id=1, source_target_pairs={{0,8},{8,16},{16,24},{24,32},{32,40},{40,48},{48,56},{56,64},{64,7... | collective-permute-start | bytes 98312 | tf_op jit(solution)/shard_map/while/body/eval_jaxpr/ppermute | solution.py:18
  74.1 6.7 %collective-permute-start = (f32[2,1,32,128]{3,2,1,0:T(8,128)S(1)}, f32[2,1,32,128]{3,2,1,0:T(8,128)S(1)}, u32[]{:S(2)}, u32[]{:S(2)}) collective-permute-start(f32[2,1,32,128]{3,2,1,0:T(8,128)S(1)} %get-tuple-element.225), channel_id=1, source_target_pairs={{8,0},{16,8},{24,16},{32,24},{40,32},{48,40},{56,48},{64,56},{72,6... | collective-permute-start | bytes 98312 | tf_op jit(solution)/shard_map/while/body/eval_jaxpr/ppermute | solution.py:21
  75.4 6.4 %collective-permute-start.1 = (f32[2,1,32,128]{3,2,1,0:T(8,128)S(1)}, f32[2,1,32,128]{3,2,1,0:T(8,128)S(1)}, u32[]{:S(2)}, u32[]{:S(2)}) collective-permute-start(f32[2,1,32,128]{3,2,1,0:T(8,128)S(1)} %get-tuple-element.226), channel_id=1, source_target_pairs={{0,8},{8,16},{16,24},{24,32},{32,40},{40,48},{48,56},{56,64},{64,7... | collective-permute-start | bytes 98312 | tf_op jit(solution)/shard_map/while/body/eval_jaxpr/ppermute | solution.py:18
  82.2 6.5 %collective-permute-start = (f32[2,1,32,128]{3,2,1,0:T(8,128)S(1)}, f32[2,1,32,128]{3,2,1,0:T(8,128)S(1)}, u32[]{:S(2)}, u32[]{:S(2)}) collective-permute-start(f32[2,1,32,128]{3,2,1,0:T(8,128)S(1)} %get-tuple-element.225), channel_id=1, source_target_pairs={{8,0},{16,8},{24,16},{32,24},{40,32},{48,40},{56,48},{64,56},{72,6... | collective-permute-start | bytes 98312 | tf_op jit(solution)/shard_map/while/body/eval_jaxpr/ppermute | solution.py:21
  83.5 6.2 %collective-permute-start.1 = (f32[2,1,32,128]{3,2,1,0:T(8,128)S(1)}, f32[2,1,32,128]{3,2,1,0:T(8,128)S(1)}, u32[]{:S(2)}, u32[]{:S(2)}) collective-permute-start(f32[2,1,32,128]{3,2,1,0:T(8,128)S(1)} %get-tuple-element.226), channel_id=1, source_target_pairs={{0,8},{8,16},{16,24},{24,32},{32,40},{40,48},{48,56},{56,64},{64,7... | collective-permute-start | bytes 98312 | tf_op jit(solution)/shard_map/while/body/eval_jaxpr/ppermute | solution.py:18
  90.2 7.9 %collective-permute-start = (f32[2,1,32,128]{3,2,1,0:T(8,128)S(1)}, f32[2,1,32,128]{3,2,1,0:T(8,128)S(1)}, u32[]{:S(2)}, u32[]{:S(2)}) collective-permute-start(f32[2,1,32,128]{3,2,1,0:T(8,128)S(1)} %get-tuple-element.225), channel_id=1, source_target_pairs={{8,0},{16,8},{24,16},{32,24},{40,32},{48,40},{56,48},{64,56},{72,6... | collective-permute-start | bytes 98312 | tf_op jit(solution)/shard_map/while/body/eval_jaxpr/ppermute | solution.py:21
  91.5 7.5 %collective-permute-start.1 = (f32[2,1,32,128]{3,2,1,0:T(8,128)S(1)}, f32[2,1,32,128]{3,2,1,0:T(8,128)S(1)}, u32[]{:S(2)}, u32[]{:S(2)}) collective-permute-start(f32[2,1,32,128]{3,2,1,0:T(8,128)S(1)} %get-tuple-element.226), channel_id=1, source_target_pairs={{0,8},{8,16},{16,24},{24,32},{32,40},{40,48},{48,56},{56,64},{64,7... | collective-permute-start | bytes 98312 | tf_op jit(solution)/shard_map/while/body/eval_jaxpr/ppermute | solution.py:18
  100.3 29.5 %all-to-all-start = ((f32[2,5,32,128]{3,0,1,2:T(2,128)}), f32[2,5,32,128]{3,0,1,2:T(2,128)S(1)}, u32[]{:S(2)}, u32[]{:S(2)}) async-start(f32[2,5,32,128]{3,0,1,2:T(2,128)} %copy.27), calls=%async_computation | async-start | bytes 327680 | tf_op jit(solution)/shard_map/all_to_all | solution.py:87
  129.8 0.7 copy-start
where the time goes:
time: 401 us; the launch traced here: 400 us
  blocking collectives  236 us (59%)
  starting transfers between devices  99.1 us (25%)
  other arithmetic  36.1 us (9%)
  waiting for transfers between devices  20.1 us (5%)
  local copies, waits for them, and re-layouts  7.41 us (2%)
    pmax x1, blocking collectives, body(): top_score = lax.pmax(local_top, ('space', 'sta'))  141 us
    psum x1, blocking collectives, body(): mass_sum = lax.psum(jnp.sum(cell_weights, 1), ('space', 'sta'))  94.4 us
    ppermute x12, starting transfers between devices, extended_2(): lax.ppermute(lax.slice_in_dim(block, block.shape[dim] - width, None, axis...  62.9 us
    all_to_all x1, starting transfers between devices, body(): lax.all_to_all(tables, 'sta', split_axis=2, concat_axis=0, tiled=True)  20.7 us
    ppermute x12, starting transfers between devices, extended_2(): lax.ppermute(lax.slice_in_dim(block, 0, width, axis=dim), axis, backward)  15.5 us
    reduce_sum x8, other arithmetic, misfit_block(): return jnp.sum(observed[:, :, None] * deviation * deviation, 1)  14 us
    ppermute x12, waiting for transfers between devices, extended_2(): lax.ppermute(lax.slice_in_dim(block, block.shape[dim] - width, None, axis...  11.5 us
    reduce_sum x8, other arithmetic, misfit_block(): jnp.sum(observed[:, :, None] * residual, 1) / pick_count[:, None]  9.54 us
  transfers between devices with their start and end apart: 25, of which 13 were waited for; matrix products, arithmetic and copies ran while one was open for 0% of the time, Pallas kernels for 0%

commit v1 on v0

--- a/solution.py
+++ b/solution.py
@@ -96,7 +96,7 @@
     local_top = jnp.max(score, 1)
     top_score = lax.pmax(local_top, ("space", "sta"))
     cell_weights = jnp.exp(score - top_score[:, None])
-    mass_sum = lax.psum(jnp.sum(cell_weights, 1), ("space", "sta"))
+    mass_sum = lax.psum(lax.psum(jnp.sum(cell_weights, 1), "sta"), "space")
     density = cell_weights / mass_sum[:, None]
     density = density.reshape(picks.shape[0], refined.shape[1], refined.shape[2], refined.shape[3])
     return (refined, density)

time: 401 us -> 475 us (1.18)
  the two profiles are of different devices: /device:TPU:1 before, /device:TPU:8 now
where the time goes in v1:
time: 475 us; the launch traced here: 474 us
  blocking collectives  308 us (65%)
  starting transfers between devices  90.2 us (19%)
  other arithmetic  36.1 us (8%)
  waiting for transfers between devices  29.7 us (6%)
  local copies, waits for them, and re-layouts  7.41 us (2%)
    psum x2, blocking collectives, body(): mass_sum = lax.psum(lax.psum(jnp.sum(cell_weights, 1), 'sta'), 'space')  170 us
    pmax x1, blocking collectives, body(): top_score = lax.pmax(local_top, ('space', 'sta'))  138 us
    ppermute x12, starting transfers between devices, extended_2(): lax.ppermute(lax.slice_in_dim(block, block.shape[dim] - width, None, axis...  58 us
    ppermute x12, starting transfers between devices, extended_2(): lax.ppermute(lax.slice_in_dim(block, 0, width, axis=dim), axis, backward)  28.8 us
    ppermute x12, waiting for transfers between devices, extended_2(): lax.ppermute(lax.slice_in_dim(block, block.shape[dim] - width, None, axis...  20.5 us
    reduce_sum x8, other arithmetic, misfit_block(): return jnp.sum(observed[:, :, None] * deviation * deviation, 1)  14 us
    reduce_sum x8, other arithmetic, misfit_block(): jnp.sum(observed[:, :, None] * residual, 1) / pick_count[:, None]  9.54 us
  transfers between devices with their start and end apart: 25, of which 14 were waited for; matrix products, arithmetic and copies ran while one was open for 0% of the time, Pallas kernels for 0%

profile of v1, /device:TPU:8, one launch (start us, length us, event | category | flops | bytes accessed | tf_op | source)
XLA Modules:
  0.0 473.6 jit_solution(6114138409365929694)
XLA Ops:
  3.1 114.0 %while.22 = (s32[]{:T(128)}, f32[2,5,32,128]{3,2,1,0:T(8,128)S(1)}, pred[]{:T(512)}, pred[]{:T(512)}, f32[5,32,128]{2,1,0:T(8,128)S(1)}, /*index=5*/f32[1,5,32,128]{3,2,1,0:T(8,128)S(1)}, s32[]{:T(128)}) while((s32[]{:T(128)}, f32[2,5,32,128]{3,2,1,0:T(8,128)S(1)}, pred[]{:T(512)}, pred[]{:T(512)}, f32[5,32,128]{2,1,0:T(8,128)S(1)}, ...), condition=%wide.region_2.3_spmd, body=%wide.region_1.2_spmd.sunk | while | flops 1523749 | bytes 2244781 | solution.py:86
  3.1 7.7 %collective-permute-start = (f32[2,1,32,128]{3,2,1,0:T(8,128)S(1)}, f32[2,1,32,128]{3,2,1,0:T(8,128)S(1)}, u32[]{:S(2)}, u32[]{:S(2)}) collective-permute-start(f32[2,1,32,128]{3,2,1,0:T(8,128)S(1)} %get-tuple-element.225), channel_id=1, source_target_pairs={{8,0},{16,8},{24,16},{32,24},{40,32},{48,40},{56,48},{64,56},{72,6... | collective-permute-start | bytes 98312 | tf_op jit(solution)/shard_map/while/body/eval_jaxpr/ppermute | solution.py:21
  10.8 1.9 collective-permute-start.1
  12.8 3.8 collective-permute-done.1
  17.1 1.9 collective-permute-start
  19.0 4.8 %collective-permute-start.1 = (f32[2,1,32,128]{3,2,1,0:T(8,128)S(1)}, f32[2,1,32,128]{3,2,1,0:T(8,128)S(1)}, u32[]{:S(2)}, u32[]{:S(2)}) collective-permute-start(f32[2,1,32,128]{3,2,1,0:T(8,128)S(1)} %get-tuple-element.226), channel_id=1, source_target_pairs={{0,8},{8,16},{16,24},{24,32},{32,40},{40,48},{48,56},{56,64},{64,7... | collective-permute-start | bytes 98312 | tf_op jit(solution)/shard_map/while/body/eval_jaxpr/ppermute | solution.py:18
  25.9 1.9 collective-permute-start
  27.9 5.1 %collective-permute-start.1 = (f32[2,1,32,128]{3,2,1,0:T(8,128)S(1)}, f32[2,1,32,128]{3,2,1,0:T(8,128)S(1)}, u32[]{:S(2)}, u32[]{:S(2)}) collective-permute-start(f32[2,1,32,128]{3,2,1,0:T(8,128)S(1)} %get-tuple-element.226), channel_id=1, source_target_pairs={{0,8},{8,16},{16,24},{24,32},{32,40},{40,48},{48,56},{56,64},{64,7... | collective-permute-start | bytes 98312 | tf_op jit(solution)/shard_map/while/body/eval_jaxpr/ppermute | solution.py:18
  35.0 1.9 collective-permute-start
  37.0 5.1 %collective-permute-start.1 = (f32[2,1,32,128]{3,2,1,0:T(8,128)S(1)}, f32[2,1,32,128]{3,2,1,0:T(8,128)S(1)}, u32[]{:S(2)}, u32[]{:S(2)}) collective-permute-start(f32[2,1,32,128]{3,2,1,0:T(8,128)S(1)} %get-tuple-element.226), channel_id=1, source_target_pairs={{0,8},{8,16},{16,24},{24,32},{32,40},{40,48},{48,56},{56,64},{64,7... | collective-permute-start | bytes 98312 | tf_op jit(solution)/shard_map/while/body/eval_jaxpr/ppermute | solution.py:18
  44.2 1.9 collective-permute-start
  46.1 5.1 %collective-permute-start.1 = (f32[2,1,32,128]{3,2,1,0:T(8,128)S(1)}, f32[2,1,32,128]{3,2,1,0:T(8,128)S(1)}, u32[]{:S(2)}, u32[]{:S(2)}) collective-permute-start(f32[2,1,32,128]{3,2,1,0:T(8,128)S(1)} %get-tuple-element.226), channel_id=1, source_target_pairs={{0,8},{8,16},{16,24},{24,32},{32,40},{40,48},{48,56},{56,64},{64,7... | collective-permute-start | bytes 98312 | tf_op jit(solution)/shard_map/while/body/eval_jaxpr/ppermute | solution.py:18
  53.3 1.9 collective-permute-start
  55.2 5.1 %collective-permute-start.1 = (f32[2,1,32,128]{3,2,1,0:T(8,128)S(1)}, f32[2,1,32,128]{3,2,1,0:T(8,128)S(1)}, u32[]{:S(2)}, u32[]{:S(2)}) collective-permute-start(f32[2,1,32,128]{3,2,1,0:T(8,128)S(1)} %get-tuple-element.226), channel_id=1, source_target_pairs={{0,8},{8,16},{16,24},{24,32},{32,40},{40,48},{48,56},{56,64},{64,7... | collective-permute-start | bytes 98312 | tf_op jit(solution)/shard_map/while/body/eval_jaxpr/ppermute | solution.py:18
  62.4 1.9 collective-permute-start
  64.3 5.1 %collective-permute-start.1 = (f32[2,1,32,128]{3,2,1,0:T(8,128)S(1)}, f32[2,1,32,128]{3,2,1,0:T(8,128)S(1)}, u32[]{:S(2)}, u32[]{:S(2)}) collective-permute-start(f32[2,1,32,128]{3,2,1,0:T(8,128)S(1)} %get-tuple-element.226), channel_id=1, source_target_pairs={{0,8},{8,16},{16,24},{24,32},{32,40},{40,48},{48,56},{56,64},{64,7... | collective-permute-start | bytes 98312 | tf_op jit(solution)/shard_map/while/body/eval_jaxpr/ppermute | solution.py:18
  71.5 1.9 collective-permute-start
  73.4 5.1 %collective-permute-start.1 = (f32[2,1,32,128]{3,2,1,0:T(8,128)S(1)}, f32[2,1,32,128]{3,2,1,0:T(8,128)S(1)}, u32[]{:S(2)}, u32[]{:S(2)}) collective-permute-start(f32[2,1,32,128]{3,2,1,0:T(8,128)S(1)} %get-tuple-element.226), channel_id=1, source_target_pairs={{0,8},{8,16},{16,24},{24,32},{32,40},{40,48},{48,56},{56,64},{64,7... | collective-permute-start | bytes 98312 | tf_op jit(solution)/shard_map/while/body/eval_jaxpr/ppermute | solution.py:18
  82.5 5.1 %collective-permute-start.1 = (f32[2,1,32,128]{3,2,1,0:T(8,128)S(1)}, f32[2,1,32,128]{3,2,1,0:T(8,128)S(1)}, u32[]{:S(2)}, u32[]{:S(2)}) collective-permute-start(f32[2,1,32,128]{3,2,1,0:T(8,128)S(1)} %get-tuple-element.226), channel_id=1, source_target_pairs={{0,8},{8,16},{16,24},{24,32},{32,40},{40,48},{48,56},{56,64},{64,7... | collective-permute-start | bytes 98312 | tf_op jit(solution)/shard_map/while/body/eval_jaxpr/ppermute | solution.py:18
  91.7 5.1 %collective-permute-start.1 = (f32[2,1,32,128]{3,2,1,0:T(8,128)S(1)}, f32[2,1,32,128]{3,2,1,0:T(8,128)S(1)}, u32[]{:S(2)}, u32[]{:S(2)}) collective-permute-start(f32[2,1,32,128]{3,2,1,0:T(8,128)S(1)} %get-tuple-element.226), channel_id=1, source_target_pairs={{0,8},{8,16},{16,24},{24,32},{32,40},{40,48},{48,56},{56,64},{64,7... | collective-permute-start | bytes 98312 | tf_op jit(solution)/shard_map/while/body/eval_jaxpr/ppermute | solution.py:18
  98.9 1.9 collective-permute-start
  100.8 5.1 %collective-permute-start.1 = (f32[2,1,32,128]{3,2,1,0:T(8,128)S(1)}, f32[2,1,32,128]{3,2,1,0:T(8,128)S(1)}, u32[]{:S(2)}, u32[]{:S(2)}) collective-permute-start(f32[2,1,32,128]{3,2,1,0:T(8,128)S(1)} %get-tuple-element.226), channel_id=1, source_target_pairs={{0,8},{8,16},{16,24},{24,32},{32,40},{40,48},{48,56},{56,64},{64,7... | collective-permute-start | bytes 98312 | tf_op jit(solution)/shard_map/while/body/eval_jaxpr/ppermute | solution.py:18
  109.9 5.1 %collective-permute-start.1 = (f32[2,1,32,128]{3,2,1,0:T(8,128)S(1)}, f32[2,1,32,128]{3,2,1,0:T(8,128)S(1)}, u32[]{:S(2)}, u32[]{:S(2)}) collective-permute-start(f32[2,1,32,128]{3,2,1,0:T(8,128)S(1)} %get-tuple-element.226), channel_id=1, source_target_pairs={{0,8},{8,16},{16,24},{24,32},{32,40},{40,48},{48,56},{56,64},{64,7... | collective-permute-start | bytes 98312 | tf_op jit(solution)/shard_map/while/body/eval_jaxpr/ppermute | solution.py:18
  117.9 3.4 all-to-all-start
  121.4 9.0 %all-to-all-done = f32[2,5,32,128]{3,0,1,2:T(2,128)S(1)} async-done(((f32[2,5,32,128]{3,0,1,2:T(2,128)}), f32[2,5,32,128]{3,0,1,2:T(2,128)S(1)}, u32[]{:S(2)}, u32[]{:S(2)}) %all-to-all-start) | async-done | bytes 163872 | tf_op jit(solution)/shard_map/all_to_all | solution.py:87
  131.1 26.5 %while.23 = (s32[]{:T(128)}, f32[8,32,2560]{2,1,0:T(8,128)S(1)}, f32[8,32,16]{1,0,2:T(8,128)S(1)}, f32[8,32,16]{1,0,2:T(8,128)S(1)}, f32[16,5,4,128]{3,2,1,0:T(4...) while((s32[]{:T(128)}, f32[8,32,2560]{2,1,0:T(8,128)S(1)}, f32[8,32,16]{1,0,2:T(8,128)S(1)}, ...), condition=%wide.wide.region_7.8_spmd, body=%wide.wide.region_3.7_spmd.sunk | while | flops 10404322 | bytes 2648417 | solution.py:91
  157.9 138.1 %pmax.7 = f32[256]{0:T(256)S(1)} all-reduce(f32[256]{0:T(256)S(1)} %reduce_max.12), channel_id=1, replica_groups=mesh['space'=64,'sta'=8] {'space','sta'}, use_global_device_ids=true, to_apply=%region_9.10 | all-reduce | flops 256 | bytes 2048 | tf_op jit(solution)/shard_map/pmax | solution.py:97
  296.1 2.0 exponential_reduce_fusion
  298.1 2.8 div.34
  301.0 16.3 %psum.14 = f32[256]{0:T(256)S(1)} all-reduce(f32[256]{0:T(256)S(1)} %reduce_sum.49), channel_id=1, replica_groups=mesh['space'=64,'sta'=8] {'sta'}, use_global_device_ids=true, to_apply=%region_11.12 | all-reduce | flops 256 | bytes 2048 | tf_op jit(solution)/shard_map/psum | solution.py:99
  317.3 153.7 %psum.15 = f32[256]{0:T(256)S(1)} all-reduce(f32[256]{0:T(256)S(1)} %psum.14), channel_id=1, replica_groups=mesh['space'=64,'sta'=8] {'space'}, use_global_device_ids=true, to_apply=%region_12.13 | all-reduce | flops 256 | bytes 2048 | tf_op jit(solution)/shard_map/psum | solution.py:99
  471.0 2.5 exponential_divide_fusion
  (182 shorter events, 58.8 us)
Async XLA Ops:
  3.1 118.2 %copy-start.2 = (s32[256,16]{0,1:T(8,128)S(1)}, s32[256,16]{0,1:T(8,128)}, u32[]{:S(2)}) copy-start(s32[256,16]{0,1:T(8,128)} %param.13) | copy-start | bytes 49156
  3.1 118.3 %copy-start.1 = (f32[256,16]{0,1:T(8,128)S(1)}, f32[256,16]{0,1:T(8,128)}, u32[]{:S(2)}) copy-start(f32[256,16]{0,1:T(8,128)} %param.12) | copy-start | bytes 49156
  3.1 9.7 %collective-permute-start = (f32[2,1,32,128]{3,2,1,0:T(8,128)S(1)}, f32[2,1,32,128]{3,2,1,0:T(8,128)S(1)}, u32[]{:S(2)}, u32[]{:S(2)}) collective-permute-start(f32[2,1,32,128]{3,2,1,0:T(8,128)S(1)} %get-tuple-element.225), channel_id=1, source_target_pairs={{8,0},{16,8},{24,16},{32,24},{40,32},{48,40},{56,48},{64,56},{72,6... | collective-permute-start | bytes 98312 | tf_op jit(solution)/shard_map/while/body/eval_jaxpr/ppermute | solution.py:21
  10.8 5.8 %collective-permute-start.1 = (f32[2,1,32,128]{3,2,1,0:T(8,128)S(1)}, f32[2,1,32,128]{3,2,1,0:T(8,128)S(1)}, u32[]{:S(2)}, u32[]{:S(2)}) collective-permute-start(f32[2,1,32,128]{3,2,1,0:T(8,128)S(1)} %get-tuple-element.226), channel_id=1, source_target_pairs={{0,8},{8,16},{16,24},{24,32},{32,40},{40,48},{48,56},{56,64},{64,7... | collective-permute-start | bytes 98312 | tf_op jit(solution)/shard_map/while/body/eval_jaxpr/ppermute | solution.py:18
  17.1 6.8 %collective-permute-start = (f32[2,1,32,128]{3,2,1,0:T(8,128)S(1)}, f32[2,1,32,128]{3,2,1,0:T(8,128)S(1)}, u32[]{:S(2)}, u32[]{:S(2)}) collective-permute-start(f32[2,1,32,128]{3,2,1,0:T(8,128)S(1)} %get-tuple-element.225), channel_id=1, source_target_pairs={{8,0},{16,8},{24,16},{32,24},{40,32},{48,40},{56,48},{64,56},{72,6... | collective-permute-start | bytes 98312 | tf_op jit(solution)/shard_map/while/body/eval_jaxpr/ppermute | solution.py:21
  19.0 6.4 %collective-permute-start.1 = (f32[2,1,32,128]{3,2,1,0:T(8,128)S(1)}, f32[2,1,32,128]{3,2,1,0:T(8,128)S(1)}, u32[]{:S(2)}, u32[]{:S(2)}) collective-permute-start(f32[2,1,32,128]{3,2,1,0:T(8,128)S(1)} %get-tuple-element.226), channel_id=1, source_target_pairs={{0,8},{8,16},{16,24},{24,32},{32,40},{40,48},{48,56},{56,64},{64,7... | collective-permute-start | bytes 98312 | tf_op jit(solution)/shard_map/while/body/eval_jaxpr/ppermute | solution.py:18
  25.9 7.1 %collective-permute-start = (f32[2,1,32,128]{3,2,1,0:T(8,128)S(1)}, f32[2,1,32,128]{3,2,1,0:T(8,128)S(1)}, u32[]{:S(2)}, u32[]{:S(2)}) collective-permute-start(f32[2,1,32,128]{3,2,1,0:T(8,128)S(1)} %get-tuple-element.225), channel_id=1, source_target_pairs={{8,0},{16,8},{24,16},{32,24},{40,32},{48,40},{56,48},{64,56},{72,6... | collective-permute-start | bytes 98312 | tf_op jit(solution)/shard_map/while/body/eval_jaxpr/ppermute | solution.py:21
  27.9 6.7 %collective-permute-start.1 = (f32[2,1,32,128]{3,2,1,0:T(8,128)S(1)}, f32[2,1,32,128]{3,2,1,0:T(8,128)S(1)}, u32[]{:S(2)}, u32[]{:S(2)}) collective-permute-start(f32[2,1,32,128]{3,2,1,0:T(8,128)S(1)} %get-tuple-element.226), channel_id=1, source_target_pairs={{0,8},{8,16},{16,24},{24,32},{32,40},{40,48},{48,56},{56,64},{64,7... | collective-permute-start | bytes 98312 | tf_op jit(solution)/shard_map/while/body/eval_jaxpr/ppermute | solution.py:18
  35.0 7.1 %collective-permute-start = (f32[2,1,32,128]{3,2,1,0:T(8,128)S(1)}, f32[2,1,32,128]{3,2,1,0:T(8,128)S(1)}, u32[]{:S(2)}, u32[]{:S(2)}) collective-permute-start(f32[2,1,32,128]{3,2,1,0:T(8,128)S(1)} %get-tuple-element.225), channel_id=1, source_target_pairs={{8,0},{16,8},{24,16},{32,24},{40,32},{48,40},{56,48},{64,56},{72,6... | collective-permute-start | bytes 98312 | tf_op jit(solution)/shard_map/while/body/eval_jaxpr/ppermute | solution.py:21
  37.0 6.7 %collective-permute-start.1 = (f32[2,1,32,128]{3,2,1,0:T(8,128)S(1)}, f32[2,1,32,128]{3,2,1,0:T(8,128)S(1)}, u32[]{:S(2)}, u32[]{:S(2)}) collective-permute-start(f32[2,1,32,128]{3,2,1,0:T(8,128)S(1)} %get-tuple-element.226), channel_id=1, source_target_pairs={{0,8},{8,16},{16,24},{24,32},{32,40},{40,48},{48,56},{56,64},{64,7... | collective-permute-start | bytes 98312 | tf_op jit(solution)/shard_map/while/body/eval_jaxpr/ppermute | solution.py:18
  44.2 7.1 %collective-permute-start = (f32[2,1,32,128]{3,2,1,0:T(8,128)S(1)}, f32[2,1,32,128]{3,2,1,0:T(8,128)S(1)}, u32[]{:S(2)}, u32[]{:S(2)}) collective-permute-start(f32[2,1,32,128]{3,2,1,0:T(8,128)S(1)} %get-tuple-element.225), channel_id=1, source_target_pairs={{8,0},{16,8},{24,16},{32,24},{40,32},{48,40},{56,48},{64,56},{72,6... | collective-permute-start | bytes 98312 | tf_op jit(solution)/shard_map/while/body/eval_jaxpr/ppermute | solution.py:21
  46.1 6.7 %collective-permute-start.1 = (f32[2,1,32,128]{3,2,1,0:T(8,128)S(1)}, f32[2,1,32,128]{3,2,1,0:T(8,128)S(1)}, u32[]{:S(2)}, u32[]{:S(2)}) collective-permute-start(f32[2,1,32,128]{3,2,1,0:T(8,128)S(1)} %get-tuple-element.226), channel_id=1, source_target_pairs={{0,8},{8,16},{16,24},{24,32},{32,40},{40,48},{48,56},{56,64},{64,7... | collective-permute-start | bytes 98312 | tf_op jit(solution)/shard_map/while/body/eval_jaxpr/ppermute | solution.py:18
  53.3 7.1 %collective-permute-start = (f32[2,1,32,128]{3,2,1,0:T(8,128)S(1)}, f32[2,1,32,128]{3,2,1,0:T(8,128)S(1)}, u32[]{:S(2)}, u32[]{:S(2)}) collective-permute-start(f32[2,1,32,128]{3,2,1,0:T(8,128)S(1)} %get-tuple-element.225), channel_id=1, source_target_pairs={{8,0},{16,8},{24,16},{32,24},{40,32},{48,40},{56,48},{64,56},{72,6... | collective-permute-start | bytes 98312 | tf_op jit(solution)/shard_map/while/body/eval_jaxpr/ppermute | solution.py:21
  55.2 6.7 %collective-permute-start.1 = (f32[2,1,32,128]{3,2,1,0:T(8,128)S(1)}, f32[2,1,32,128]{3,2,1,0:T(8,128)S(1)}, u32[]{:S(2)}, u32[]{:S(2)}) collective-permute-start(f32[2,1,32,128]{3,2,1,0:T(8,128)S(1)} %get-tuple-element.226), channel_id=1, source_target_pairs={{0,8},{8,16},{16,24},{24,32},{32,40},{40,48},{48,56},{56,64},{64,7... | collective-permute-start | bytes 98312 | tf_op jit(solution)/shard_map/while/body/eval_jaxpr/ppermute | solution.py:18
  62.4 7.1 %collective-permute-start = (f32[2,1,32,128]{3,2,1,0:T(8,128)S(1)}, f32[2,1,32,128]{3,2,1,0:T(8,128)S(1)}, u32[]{:S(2)}, u32[]{:S(2)}) collective-permute-start(f32[2,1,32,128]{3,2,1,0:T(8,128)S(1)} %get-tuple-element.225), channel_id=1, source_target_pairs={{8,0},{16,8},{24,16},{32,24},{40,32},{48,40},{56,48},{64,56},{72,6... | collective-permute-start | bytes 98312 | tf_op jit(solution)/shard_map/while/body/eval_jaxpr/ppermute | solution.py:21
  64.3 6.7 %collective-permute-start.1 = (f32[2,1,32,128]{3,2,1,0:T(8,128)S(1)}, f32[2,1,32,128]{3,2,1,0:T(8,128)S(1)}, u32[]{:S(2)}, u32[]{:S(2)}) collective-permute-start(f32[2,1,32,128]{3,2,1,0:T(8,128)S(1)} %get-tuple-element.226), channel_id=1, source_target_pairs={{0,8},{8,16},{16,24},{24,32},{32,40},{40,48},{48,56},{56,64},{64,7... | collective-permute-start | bytes 98312 | tf_op jit(solution)/shard_map/while/body/eval_jaxpr/ppermute | solution.py:18
  71.5 7.1 %collective-permute-start = (f32[2,1,32,128]{3,2,1,0:T(8,128)S(1)}, f32[2,1,32,128]{3,2,1,0:T(8,128)S(1)}, u32[]{:S(2)}, u32[]{:S(2)}) collective-permute-start(f32[2,1,32,128]{3,2,1,0:T(8,128)S(1)} %get-tuple-element.225), channel_id=1, source_target_pairs={{8,0},{16,8},{24,16},{32,24},{40,32},{48,40},{56,48},{64,56},{72,6... | collective-permute-start | bytes 98312 | tf_op jit(solution)/shard_map/while/body/eval_jaxpr/ppermute | solution.py:21
  73.4 6.7 %collective-permute-start.1 = (f32[2,1,32,128]{3,2,1,0:T(8,128)S(1)}, f32[2,1,32,128]{3,2,1,0:T(8,128)S(1)}, u32[]{:S(2)}, u32[]{:S(2)}) collective-permute-start(f32[2,1,32,128]{3,2,1,0:T(8,128)S(1)} %get-tuple-element.226), channel_id=1, source_target_pairs={{0,8},{8,16},{16,24},{24,32},{32,40},{40,48},{48,56},{56,64},{64,7... | collective-permute-start | bytes 98312 | tf_op jit(solution)/shard_map/while/body/eval_jaxpr/ppermute | solution.py:18
  80.6 7.1 %collective-permute-start = (f32[2,1,32,128]{3,2,1,0:T(8,128)S(1)}, f32[2,1,32,128]{3,2,1,0:T(8,128)S(1)}, u32[]{:S(2)}, u32[]{:S(2)}) collective-permute-start(f32[2,1,32,128]{3,2,1,0:T(8,128)S(1)} %get-tuple-element.225), channel_id=1, source_target_pairs={{8,0},{16,8},{24,16},{32,24},{40,32},{48,40},{56,48},{64,56},{72,6... | collective-permute-start | bytes 98312 | tf_op jit(solution)/shard_map/while/body/eval_jaxpr/ppermute | solution.py:21
  82.5 6.7 %collective-permute-start.1 = (f32[2,1,32,128]{3,2,1,0:T(8,128)S(1)}, f32[2,1,32,128]{3,2,1,0:T(8,128)S(1)}, u32[]{:S(2)}, u32[]{:S(2)}) collective-permute-start(f32[2,1,32,128]{3,2,1,0:T(8,128)S(1)} %get-tuple-element.226), channel_id=1, source_target_pairs={{0,8},{8,16},{16,24},{24,32},{32,40},{40,48},{48,56},{56,64},{64,7... | collective-permute-start | bytes 98312 | tf_op jit(solution)/shard_map/while/body/eval_jaxpr/ppermute | solution.py:18
  89.7 7.2 %collective-permute-start = (f32[2,1,32,128]{3,2,1,0:T(8,128)S(1)}, f32[2,1,32,128]{3,2,1,0:T(8,128)S(1)}, u32[]{:S(2)}, u32[]{:S(2)}) collective-permute-start(f32[2,1,32,128]{3,2,1,0:T(8,128)S(1)} %get-tuple-element.225), channel_id=1, source_target_pairs={{8,0},{16,8},{24,16},{32,24},{40,32},{48,40},{56,48},{64,56},{72,6... | collective-permute-start | bytes 98312 | tf_op jit(solution)/shard_map/while/body/eval_jaxpr/ppermute | solution.py:21
  91.7 6.7 %collective-permute-start.1 = (f32[2,1,32,128]{3,2,1,0:T(8,128)S(1)}, f32[2,1,32,128]{3,2,1,0:T(8,128)S(1)}, u32[]{:S(2)}, u32[]{:S(2)}) collective-permute-start(f32[2,1,32,128]{3,2,1,0:T(8,128)S(1)} %get-tuple-element.226), channel_id=1, source_target_pairs={{0,8},{8,16},{16,24},{24,32},{32,40},{40,48},{48,56},{56,64},{64,7... | collective-permute-start | bytes 98312 | tf_op jit(solution)/shard_map/while/body/eval_jaxpr/ppermute | solution.py:18
  98.9 7.1 %collective-permute-start = (f32[2,1,32,128]{3,2,1,0:T(8,128)S(1)}, f32[2,1,32,128]{3,2,1,0:T(8,128)S(1)}, u32[]{:S(2)}, u32[]{:S(2)}) collective-permute-start(f32[2,1,32,128]{3,2,1,0:T(8,128)S(1)} %get-tuple-element.225), channel_id=1, source_target_pairs={{8,0},{16,8},{24,16},{32,24},{40,32},{48,40},{56,48},{64,56},{72,6... | collective-permute-start | bytes 98312 | tf_op jit(solution)/shard_map/while/body/eval_jaxpr/ppermute | solution.py:21
  100.8 6.7 %collective-permute-start.1 = (f32[2,1,32,128]{3,2,1,0:T(8,128)S(1)}, f32[2,1,32,128]{3,2,1,0:T(8,128)S(1)}, u32[]{:S(2)}, u32[]{:S(2)}) collective-permute-start(f32[2,1,32,128]{3,2,1,0:T(8,128)S(1)} %get-tuple-element.226), channel_id=1, source_target_pairs={{0,8},{8,16},{16,24},{24,32},{32,40},{40,48},{48,56},{56,64},{64,7... | collective-permute-start | bytes 98312 | tf_op jit(solution)/shard_map/while/body/eval_jaxpr/ppermute | solution.py:18
  108.0 7.1 %collective-permute-start = (f32[2,1,32,128]{3,2,1,0:T(8,128)S(1)}, f32[2,1,32,128]{3,2,1,0:T(8,128)S(1)}, u32[]{:S(2)}, u32[]{:S(2)}) collective-permute-start(f32[2,1,32,128]{3,2,1,0:T(8,128)S(1)} %get-tuple-element.225), channel_id=1, source_target_pairs={{8,0},{16,8},{24,16},{32,24},{40,32},{48,40},{56,48},{64,56},{72,6... | collective-permute-start | bytes 98312 | tf_op jit(solution)/shard_map/while/body/eval_jaxpr/ppermute | solution.py:21
  109.9 6.7 %collective-permute-start.1 = (f32[2,1,32,128]{3,2,1,0:T(8,128)S(1)}, f32[2,1,32,128]{3,2,1,0:T(8,128)S(1)}, u32[]{:S(2)}, u32[]{:S(2)}) collective-permute-start(f32[2,1,32,128]{3,2,1,0:T(8,128)S(1)} %get-tuple-element.226), channel_id=1, source_target_pairs={{0,8},{8,16},{16,24},{24,32},{32,40},{40,48},{48,56},{56,64},{64,7... | collective-permute-start | bytes 98312 | tf_op jit(solution)/shard_map/while/body/eval_jaxpr/ppermute | solution.py:18
  117.9 12.5 %all-to-all-start = ((f32[2,5,32,128]{3,0,1,2:T(2,128)}), f32[2,5,32,128]{3,0,1,2:T(2,128)S(1)}, u32[]{:S(2)}, u32[]{:S(2)}) async-start(f32[2,5,32,128]{3,0,1,2:T(2,128)} %copy.27), calls=%async_computation | async-start | bytes 327680 | tf_op jit(solution)/shard_map/all_to_all | solution.py:87
  130.4 0.7 copy-start
